TPU v7x, 512 devices: a whole 4x8x8 slice. The times are simulated.
512 devices in a mesh: harm: 32 (over y_lo, z), slab: 16 (over y_hi, x, core).
Axes of the slice: x: 4, y: 8 (y_hi: 2, y_lo: 4; y = y_hi * 4 + y_lo), z: 8, core: 2. Of those that a mesh axis runs over, the one named last changes fastest.
Arguments:
- fields: bfloat16 [64, 4, 2, 5, 128, 256], P('harm', None, None, None, 'slab'), may hold values from -6 to 6
- base_store: bfloat16 [32, 2, 5, 128, 256], P('harm', None, None, 'slab'), may hold values from -3 to 3
- harmonic_index: int32 [3], replicated, may hold values from 1 to 63
- owners: int32 [3], replicated, may hold values from 0 to 31
- sponge_flags: int32 [128], P('slab'), may hold values 0 or 1
- mixing: float32 [5, 5], replicated, may hold values from -2.5 to 2.5
Outputs:
- applied: bfloat16 [64, 4, 2, 5, 128, 256], P('harm', None, None, None, 'slab')
Inputs may be any that keep to these rules, and one draw needn't show every extreme that they name: `harmonic_index`: indices of the coupling base-flow harmonics, taken modulo 64.
All inputs are finite; a program needn't handle non-finite values. No bound on the sum of `sponge_flags` on one device may be relied on, other than what follows from the above.
Results may differ from a plain program's by a relative error of at most 0.0075.
Values may be sent and summed in bfloat16 or wider, within the bound.
A program may use at most 64 MiB of HBM per device.

v0:
```python
import jax
import jax.numpy as jnp
from jax import lax
from jax.sharding import PartitionSpec as P

NH = 64
NBASE = 3


coeffs = (0.75, -0.15, 1.0 / 60.0)


def shifted_2(value, axis, by):
    size = lax.axis_size(axis)
    return lax.ppermute(value, axis, [(i, (i + by) % size) for i in range(size)])


def with_halo(cells, sides, width):
    for axis, dim in sides:
        count = lax.axis_size(axis)
        head = lax.slice_in_dim(cells, 0, width, axis=dim)
        tail = lax.slice_in_dim(cells, cells.shape[dim] - width, cells.shape[dim], axis=dim)
        cells = jnp.concatenate(
            [
                lax.ppermute(tail, axis, [(i, (i + 1) % count) for i in range(count)]),
                cells,
                lax.ppermute(head, axis, [((i + 1) % count, i) for i in range(count)]),
            ],
            axis=dim,
        )
    return cells


def spread(value, axis, root):
    mine = lax.axis_index(axis) == root
    return lax.psum(jnp.where(mine, value, jnp.zeros_like(value)), axis)


def mix_block(source, mixing, width):
    xaxis = source.ndim - 2
    center = lax.slice_in_dim(source, 3, 3 + width, axis=xaxis).astype(jnp.float32)
    total = jnp.zeros(center.shape, jnp.float32)
    for shift_by in range(1, 4):
        weight = coeffs[shift_by - 1]
        upper = lax.slice_in_dim(source, 3 + shift_by, 3 + shift_by + width, axis=xaxis).astype(
            jnp.float32
        )
        lower = lax.slice_in_dim(source, 3 - shift_by, 3 - shift_by + width, axis=xaxis).astype(
            jnp.float32
        )
        total = total + weight * (upper - lower)
        total = total + weight * (
            jnp.roll(center, -shift_by, axis=xaxis + 1) - jnp.roll(center, shift_by, axis=xaxis + 1)
        )
    mixed = jnp.einsum("vw,...wxz->...vxz", mixing, total, precision=lax.Precision.HIGHEST)
    return mixed.astype(jnp.bfloat16)


def coupling(mixed_bf, base):
    mixed = mixed_bf.astype(jnp.float32)
    base_real = base[0].astype(jnp.float32)
    base_imag = base[1].astype(jnp.float32)
    real_part = base_real * mixed[:, :, 0] - base_imag * mixed[:, :, 1]
    imag_part = base_real * mixed[:, :, 1] + base_imag * mixed[:, :, 0]
    return (real_part, imag_part)


def rotate(stack, steps_whole, digits):
    current = stack
    for digit in range(digits):
        moved = shifted_2(current, "harm", 1 << digit)
        taken = steps_whole >> digit & 1 == 1
        taken = taken.reshape((-1,) + (1,) * (current.ndim - 1))
        current = jnp.where(taken, moved, current)
    return current


def assemble(current, leftover, count):
    prior = shifted_2(current, "harm", 1)
    starts = count - leftover
    joined = jnp.concatenate([prior, current], axis=1)
    return jax.vmap(lambda block, start: lax.dynamic_slice_in_dim(block, start, count, 0))(
        joined, starts
    )


def body(fields, base_store, harmonic_index, owners, sponge_flags, mixing):
    count = fields.shape[0]
    width = fields.shape[4]
    padded = with_halo(fields, (("slab", 4),), 3)
    bases = [spread(base_store[0], "harm", owners[j]) for j in range(NBASE)]
    digits = lax.axis_size("harm").bit_length() - 1
    steps_whole = harmonic_index // count
    leftover = harmonic_index % count
    global_index = lax.axis_index("harm") * count + jnp.arange(count, dtype=jnp.int32)
    shifted = [
        assemble(rotate(padded[None], steps_whole[j : j + 1], digits), leftover[j : j + 1], count)[
            0
        ]
        for j in range(NBASE)
    ]
    mixed_list = [mix_block(piece, mixing, width) for piece in shifted]
    local = fields.astype(jnp.float32)
    freq = 0.1 * jnp.where(global_index < NH // 2, global_index, global_index - NH).astype(
        jnp.float32
    )
    freq = freq.reshape((count, 1, 1, 1, 1))
    flags = sponge_flags.astype(jnp.float32).reshape((width, 1))
    real_part = -freq * local[:, :, 1] - 2.0 * flags * local[:, :, 0]
    imag_part = freq * local[:, :, 0] - 2.0 * flags * local[:, :, 1]
    for j in range(NBASE):
        term_real, term_imag = coupling(mixed_list[j], bases[j])
        real_part = real_part + term_real
        imag_part = imag_part + term_imag
    return jnp.stack([real_part, imag_part], axis=2).astype(jnp.bfloat16)


def solution(mesh):
    return jax.shard_map(
        body,
        mesh=mesh,
        in_specs=(
            P("harm", None, None, None, "slab", None),
            P("harm", None, None, "slab", None),
            P(),
            P(),
            P("slab"),
            P(),
        ),
        out_specs=P("harm", None, None, None, "slab", None),
        check_vma=False,
    )
```

profile of v0, /device:TPU:8, one launch (start us, length us, event | category | flops | bytes accessed | tf_op | source)
XLA Modules:
  0.0 572.4 jit_solution(10747174082398474315)
XLA Ops:
  6.5 1.2 copy.48
  7.8 1.9 collective-permute-start
  9.7 9.7 %collective-permute-start.1 = (bf16[2,4,2,5,3,256]{5,1,4,3,2,0:T(4,128)(2,1)S(1)}, bf16[2,4,2,5,3,256]{5,1,4,3,2,0:T(4,128)(2,1)S(1)}, u32[]{:S(2)}, u32[]{:S(2)}) collective-permute-start(bf16[2,4,2,5,3,256]{5,1,4,3,2,0:T(4,128)(2,1)S(1)} %get-tuple-element.102), channel_id=1, source_target_pairs={{1,0},{2,1},{3,2},{4,3},{5,4},{6,5},{7,6},{8,7},{9,8},{10,9},{11,1... | collective-permute-start | bytes 368648 | tf_op jit(solution)/shard_map/ppermute | solution.py:27
  19.4 0.7 collective-permute-done
  20.1 1.7 collective-permute-done.1
  21.8 0.4 maximum_bitcast_fusion
  22.2 4.3 collective-permute-start.2
  26.6 0.6 fusion.71
  29.0 16.1 %collective-permute-done.2 = bf16[1,2,4,2,5,14,256]{6,2,5,4,3,1,0:T(4,128)(2,1)S(1)} collective-permute-done((bf16[1,2,4,2,5,14,256]{6,2,5,4,3,1,0:T(4,128)(2,1)S(1)}, bf16[1,2,4,2,5,14,256]{6,2,5,4,3,1,0:T(4,128)(2,1)S(1)}, u32[]{:S(2)}, u32[]{:S(2)}) %collective-permute-start.2) | collective-permute-done | bytes 573472 | tf_op jit(solution)/shard_map/ppermute | solution.py:15
  45.1 0.9 broadcast_select_fusion.10
  46.0 1.9 collective-permute-start.3
  47.9 0.6 fusion.70
  50.4 0.6 select_bitcast_fusion.2
  51.0 2.6 collective-permute-start.8
  54.4 3.1 collective-permute-start.13
  57.5 23.0 %collective-permute-done.3 = bf16[1,2,4,2,5,14,256]{6,2,5,4,3,1,0:T(4,128)(2,1)} collective-permute-done((bf16[1,2,4,2,5,14,256]{6,2,5,4,3,1,0:T(4,128)(2,1)S(1)}, bf16[1,2,4,2,5,14,256]{6,2,5,4,3,1,0:T(4,128)(2,1)}, u32[]{:S(2)}, u32[]{:S(2)}) %collective-permute-start.3) | collective-permute-done | bytes 573472 | tf_op jit(solution)/shard_map/ppermute | solution.py:15
  80.6 1.9 collective-permute-start.4
  84.4 35.3 %collective-permute-done.8 = bf16[1,2,4,2,5,14,256]{6,2,5,4,3,1,0:T(4,128)(2,1)} collective-permute-done((bf16[1,2,4,2,5,14,256]{6,2,5,4,3,1,0:T(4,128)(2,1)S(1)}, bf16[1,2,4,2,5,14,256]{6,2,5,4,3,1,0:T(4,128)(2,1)}, u32[]{:S(2)}, u32[]{:S(2)}) %collective-permute-start.8) | collective-permute-done | bytes 573472 | tf_op jit(solution)/shard_map/ppermute | solution.py:15
  119.6 1.1 broadcast_select_fusion.6
  120.8 11.6 %collective-permute-start.9 = (bf16[1,2,4,2,5,14,256]{6,2,5,4,3,1,0:T(4,128)(2,1)S(1)}, bf16[1,2,4,2,5,14,256]{6,2,5,4,3,1,0:T(4,128)(2,1)S(1)}, u32[]{:S(2)}, u32[]{:S(2)}) collective-permute-start(bf16[1,2,4,2,5,14,256]{6,2,5,4,3,1,0:T(4,128)(2,1)S(1)} %bitcast.128), channel_id=1, source_target_pairs={{0,64},{16,80},{32,96},{48,112},{64,128},{80,144},{96,160},{112,17... | collective-permute-start | bytes 1720328 | tf_op jit(solution)/shard_map/ppermute | solution.py:15
  132.4 1.6 collective-permute-done.13
  134.1 20.7 %collective-permute-start.14 = (bf16[1,2,4,2,5,14,256]{6,2,5,4,3,1,0:T(4,128)(2,1)S(1)}, bf16[1,2,4,2,5,14,256]{6,2,5,4,3,1,0:T(4,128)(2,1)S(1)}, u32[]{:S(2)}, u32[]{:S(2)}) collective-permute-start(bf16[1,2,4,2,5,14,256]{6,2,5,4,3,1,0:T(4,128)(2,1)S(1)} %bitcast.129), channel_id=1, source_target_pairs={{0,64},{16,80},{32,96},{48,112},{64,128},{80,144},{96,160},{112,17... | collective-permute-start | bytes 1720328 | tf_op jit(solution)/shard_map/ppermute | solution.py:15
  154.8 1.1 broadcast_select_fusion.12
  156.0 27.7 %collective-permute-start.5 = (bf16[1,2,4,2,5,14,256]{6,2,5,4,3,1,0:T(4,128)(2,1)S(1)}, bf16[1,2,4,2,5,14,256]{6,2,5,4,3,1,0:T(4,128)(2,1)S(1)}, u32[]{:S(2)}, u32[]{:S(2)}) collective-permute-start(bf16[1,2,4,2,5,14,256]{6,2,5,4,3,1,0:T(4,128)(2,1)S(1)} %bitcast.130), channel_id=1, source_target_pairs={{0,128},{16,144},{32,160},{48,176},{64,192},{80,208},{96,224},{112... | collective-permute-start | bytes 1720328 | tf_op jit(solution)/shard_map/ppermute | solution.py:15
  192.2 10.1 %collective-permute-start.10 = (bf16[1,2,4,2,5,14,256]{6,2,5,4,3,1,0:T(4,128)(2,1)S(1)}, bf16[1,2,4,2,5,14,256]{6,2,5,4,3,1,0:T(4,128)(2,1)S(1)}, u32[]{:S(2)}, u32[]{:S(2)}) collective-permute-start(bf16[1,2,4,2,5,14,256]{6,2,5,4,3,1,0:T(4,128)(2,1)S(1)} %bitcast.143), channel_id=1, source_target_pairs={{0,128},{16,144},{32,160},{48,176},{64,192},{80,208},{96,224},{112... | collective-permute-start | bytes 1720328 | tf_op jit(solution)/shard_map/ppermute | solution.py:15
  202.3 19.7 %collective-permute-done.14 = bf16[1,2,4,2,5,14,256]{6,2,5,4,3,1,0:T(4,128)(2,1)S(1)} collective-permute-done((bf16[1,2,4,2,5,14,256]{6,2,5,4,3,1,0:T(4,128)(2,1)S(1)}, bf16[1,2,4,2,5,14,256]{6,2,5,4,3,1,0:T(4,128)(2,1)S(1)}, u32[]{:S(2)}, u32[]{:S(2)}) %collective-permute-start.14) | collective-permute-done | bytes 573472 | tf_op jit(solution)/shard_map/ppermute | solution.py:15
  222.0 1.9 collective-permute-start.15
  224.0 1.9 collective-permute-start.6
  226.0 233.4 %all-reduce.3.cloned.1.call-done = (bf16[2,5,8,256]{3,2,1,0:T(8,128)(2,1)}, bf16[2,5,8,256]{3,2,1,0:T(8,128)(2,1)}, bf16[2,5,8,256]{3,2,1,0:T(8,128)(2,1)}) async-done(((bf16[2,5,8,256]{3,2,1,0:T(8,128)(2,1)}, bf16[2,5,8,256]{3,2,1,0:T(8,128)(2,1)}, bf16[2,5,8,256]{3,2,1,0:T(8,128)(2,1)}), (bf16[2,5,8,256]{3,2,1,0:T(8,128)(2,1)}, bf16[2,5,8,256]{3,2,1,0:T(8,128)(2,1)}, ...) | async-done | bytes 122896 | tf_op jit(solution)/shard_map/psum | solution.py:36
  459.4 0.8 fusion.37
  460.3 1.9 collective-permute-start.11
  462.2 1.1 broadcast_select_fusion.3
  463.4 4.8 collective-permute-start.16
  468.2 1.1 broadcast_select_fusion.14
  469.4 2.3 collective-permute-start.7
  471.8 16.1 %collective-permute-done.11 = bf16[1,2,4,2,5,14,256]{6,2,5,4,3,1,0:T(4,128)(2,1)S(1)} collective-permute-done((bf16[1,2,4,2,5,14,256]{6,2,5,4,3,1,0:T(4,128)(2,1)S(1)}, bf16[1,2,4,2,5,14,256]{6,2,5,4,3,1,0:T(4,128)(2,1)S(1)}, u32[]{:S(2)}, u32[]{:S(2)}) %collective-permute-start.11) | collective-permute-done | bytes 573472 | tf_op jit(solution)/shard_map/ppermute | solution.py:15
  488.0 1.9 collective-permute-start.12
  489.9 5.7 %collective-permute-done.16 = bf16[1,2,4,2,5,14,256]{6,2,5,4,3,1,0:T(4,128)(2,1)S(1)} collective-permute-done((bf16[1,2,4,2,5,14,256]{6,2,5,4,3,1,0:T(4,128)(2,1)S(1)}, bf16[1,2,4,2,5,14,256]{6,2,5,4,3,1,0:T(4,128)(2,1)S(1)}, u32[]{:S(2)}, u32[]{:S(2)}) %collective-permute-start.16) | collective-permute-done | bytes 573472 | tf_op jit(solution)/shard_map/ppermute | solution.py:15
  495.7 2.1 collective-permute-start.17
  497.8 0.7 fusion.35
  498.6 0.4 copy.139
  499.0 1.9 fusion.66
  501.7 0.2 fusion.51
  502.0 0.2 fusion.53
  502.2 44.1 %collective-permute-done.12 = bf16[1,2,4,2,5,14,256]{6,2,5,4,3,1,0:T(4,128)(2,1)S(1)} collective-permute-done((bf16[1,2,4,2,5,14,256]{6,2,5,4,3,1,0:T(4,128)(2,1)S(1)}, bf16[1,2,4,2,5,14,256]{6,2,5,4,3,1,0:T(4,128)(2,1)S(1)}, u32[]{:S(2)}, u32[]{:S(2)}) %collective-permute-start.12) | collective-permute-done | bytes 573472 | tf_op jit(solution)/shard_map/ppermute | solution.py:15
  546.3 0.7 fusion.34
  547.0 0.4 copy.138
  547.5 1.9 fusion.67
  550.4 0.2 fusion.59
  550.6 1.8 collective-permute-done.17
  552.4 0.7 fusion.33
  553.1 0.4 copy.137
  553.6 2.1 fusion.68
  556.1 0.2 fusion.63
  556.3 0.2 fusion.65
  557.0 1.0 fusion.14
  558.0 1.2 fusion.1
  559.2 1.0 fusion.22
  560.1 1.2 fusion.3
  561.4 1.0 fusion.30
  562.3 1.2 fusion.5
  563.5 0.6 add_convert_fusion.1
  564.1 0.5 add_convert_fusion
  564.7 0.8 copy.83
  (60 shorter events, 3.6 us)
Async XLA Ops:
  6.5 551.4 %copy-start = (f32[5,5]{1,0:T(8,128)S(1)}, f32[5,5]{1,0:T(8,128)}, u32[]{:S(2)}) copy-start(f32[5,5]{1,0:T(8,128)} %param.11) | copy-start | bytes 304
  6.5 20.0 %copy-start.5 = (s32[3]{0:T(128)S(1)}, s32[3]{0:T(128)}, u32[]{:S(2)}) copy-start(s32[3]{0:T(128)} %param.8) | copy-start | bytes 40
  6.5 452.9 %all-reduce.3.cloned.1.call-start = ((), (), s32[]{:S(2)}) async-start(), calls=%async_computation | async-start | bytes 245760 | tf_op jit(solution)/shard_map/psum | solution.py:36
  7.8 12.3 %collective-permute-start = (bf16[2,4,2,5,3,256]{5,1,4,3,2,0:T(4,128)(2,1)S(1)}, bf16[2,4,2,5,3,256]{5,1,4,3,2,0:T(4,128)(2,1)S(1)}, u32[]{:S(2)}, u32[]{:S(2)}) collective-permute-start(bf16[2,4,2,5,3,256]{5,1,4,3,2,0:T(4,128)(2,1)S(1)} %get-tuple-element.101), channel_id=1, source_target_pairs={{0,1},{1,2},{2,3},{3,4},{4,5},{5,6},{6,7},{7,8},{8,9},{9,10},{10,1... | collective-permute-start | bytes 368648 | tf_op jit(solution)/shard_map/ppermute | solution.py:25
  9.7 12.1 %collective-permute-start.1 = (bf16[2,4,2,5,3,256]{5,1,4,3,2,0:T(4,128)(2,1)S(1)}, bf16[2,4,2,5,3,256]{5,1,4,3,2,0:T(4,128)(2,1)S(1)}, u32[]{:S(2)}, u32[]{:S(2)}) collective-permute-start(bf16[2,4,2,5,3,256]{5,1,4,3,2,0:T(4,128)(2,1)S(1)} %get-tuple-element.102), channel_id=1, source_target_pairs={{1,0},{2,1},{3,2},{4,3},{5,4},{6,5},{7,6},{8,7},{9,8},{10,9},{11,1... | collective-permute-start | bytes 368648 | tf_op jit(solution)/shard_map/ppermute | solution.py:27
  22.2 22.9 %collective-permute-start.2 = (bf16[1,2,4,2,5,14,256]{6,2,5,4,3,1,0:T(4,128)(2,1)S(1)}, bf16[1,2,4,2,5,14,256]{6,2,5,4,3,1,0:T(4,128)(2,1)S(1)}, u32[]{:S(2)}, u32[]{:S(2)}) collective-permute-start(bf16[1,2,4,2,5,14,256]{6,2,5,4,3,1,0:T(4,128)(2,1)S(1)} %maximum_bitcast_fusion), channel_id=1, source_target_pairs={{0,16},{16,32},{32,48},{48,64},{64,80},{80,96},{96,112},{112,128},... | collective-permute-start | bytes 1720328 | tf_op jit(solution)/shard_map/ppermute | solution.py:15
  45.1 2.8 copy-start.4
  45.1 5.3 copy-start.2
  45.1 8.6 %copy-start.1 = (bf16[2,4,2,5,8,256]{5,4,3,2,1,0:T(8,128)(2,1)S(1)}, bf16[2,4,2,5,8,256]{5,4,3,2,1,0:T(8,128)(2,1)}, u32[]{:S(2)}) copy-start(bf16[2,4,2,5,8,256]{5,4,3,2,1,0:T(8,128)(2,1)} %param.6) | copy-start | bytes 983044
  46.0 34.5 %collective-permute-start.3 = (bf16[1,2,4,2,5,14,256]{6,2,5,4,3,1,0:T(4,128)(2,1)S(1)}, bf16[1,2,4,2,5,14,256]{6,2,5,4,3,1,0:T(4,128)(2,1)}, u32[]{:S(2)}, u32[]{:S(2)}) collective-permute-start(bf16[1,2,4,2,5,14,256]{6,2,5,4,3,1,0:T(4,128)(2,1)S(1)} %get-tuple-element.41), channel_id=1, source_target_pairs={{0,32},{16,48},{32,64},{48,80},{64,96},{80,112},{96,128},{112,144}... | collective-permute-start | bytes 1720328 | tf_op jit(solution)/shard_map/ppermute | solution.py:15
  51.0 68.6 %collective-permute-start.8 = (bf16[1,2,4,2,5,14,256]{6,2,5,4,3,1,0:T(4,128)(2,1)S(1)}, bf16[1,2,4,2,5,14,256]{6,2,5,4,3,1,0:T(4,128)(2,1)}, u32[]{:S(2)}, u32[]{:S(2)}) collective-permute-start(bf16[1,2,4,2,5,14,256]{6,2,5,4,3,1,0:T(4,128)(2,1)S(1)} %get-tuple-element.43), channel_id=1, source_target_pairs={{0,32},{16,48},{32,64},{48,80},{64,96},{80,112},{96,128},{112,144}... | collective-permute-start | bytes 1720328 | tf_op jit(solution)/shard_map/ppermute | solution.py:15
  53.8 28.7 %copy-start.6 = (s32[8]{0:T(128)S(1)}, s32[8]{0:T(128)}, u32[]{:S(2)}) copy-start(s32[8]{0:T(128)} %param.10) | copy-start | bytes 100
  54.4 79.6 %collective-permute-start.13 = (bf16[1,2,4,2,5,14,256]{6,2,5,4,3,1,0:T(4,128)(2,1)S(1)}, bf16[1,2,4,2,5,14,256]{6,2,5,4,3,1,0:T(4,128)(2,1)}, u32[]{:S(2)}, u32[]{:S(2)}) collective-permute-start(bf16[1,2,4,2,5,14,256]{6,2,5,4,3,1,0:T(4,128)(2,1)S(1)} %get-tuple-element.42), channel_id=1, source_target_pairs={{0,32},{16,48},{32,64},{48,80},{64,96},{80,112},{96,128},{112,144}... | collective-permute-start | bytes 1720328 | tf_op jit(solution)/shard_map/ppermute | solution.py:15
  80.6 74.2 %collective-permute-start.4 = (bf16[1,2,4,2,5,14,256]{6,2,5,4,3,1,0:T(4,128)(2,1)S(1)}, bf16[1,2,4,2,5,14,256]{6,2,5,4,3,1,0:T(4,128)(2,1)}, u32[]{:S(2)}, u32[]{:S(2)}) collective-permute-start(bf16[1,2,4,2,5,14,256]{6,2,5,4,3,1,0:T(4,128)(2,1)S(1)} %bitcast.142), channel_id=1, source_target_pairs={{0,64},{16,80},{32,96},{48,112},{64,128},{80,144},{96,160},{112,17... | collective-permute-start | bytes 1720328 | tf_op jit(solution)/shard_map/ppermute | solution.py:15
  120.8 71.3 %collective-permute-start.9 = (bf16[1,2,4,2,5,14,256]{6,2,5,4,3,1,0:T(4,128)(2,1)S(1)}, bf16[1,2,4,2,5,14,256]{6,2,5,4,3,1,0:T(4,128)(2,1)S(1)}, u32[]{:S(2)}, u32[]{:S(2)}) collective-permute-start(bf16[1,2,4,2,5,14,256]{6,2,5,4,3,1,0:T(4,128)(2,1)S(1)} %bitcast.128), channel_id=1, source_target_pairs={{0,64},{16,80},{32,96},{48,112},{64,128},{80,144},{96,160},{112,17... | collective-permute-start | bytes 1720328 | tf_op jit(solution)/shard_map/ppermute | solution.py:15
  134.1 87.9 %collective-permute-start.14 = (bf16[1,2,4,2,5,14,256]{6,2,5,4,3,1,0:T(4,128)(2,1)S(1)}, bf16[1,2,4,2,5,14,256]{6,2,5,4,3,1,0:T(4,128)(2,1)S(1)}, u32[]{:S(2)}, u32[]{:S(2)}) collective-permute-start(bf16[1,2,4,2,5,14,256]{6,2,5,4,3,1,0:T(4,128)(2,1)S(1)} %bitcast.129), channel_id=1, source_target_pairs={{0,64},{16,80},{32,96},{48,112},{64,128},{80,144},{96,160},{112,17... | collective-permute-start | bytes 1720328 | tf_op jit(solution)/shard_map/ppermute | solution.py:15
  156.0 68.0 %collective-permute-start.5 = (bf16[1,2,4,2,5,14,256]{6,2,5,4,3,1,0:T(4,128)(2,1)S(1)}, bf16[1,2,4,2,5,14,256]{6,2,5,4,3,1,0:T(4,128)(2,1)S(1)}, u32[]{:S(2)}, u32[]{:S(2)}) collective-permute-start(bf16[1,2,4,2,5,14,256]{6,2,5,4,3,1,0:T(4,128)(2,1)S(1)} %bitcast.130), channel_id=1, source_target_pairs={{0,128},{16,144},{32,160},{48,176},{64,192},{80,208},{96,224},{112... | collective-permute-start | bytes 1720328 | tf_op jit(solution)/shard_map/ppermute | solution.py:15
  192.2 268.0 %collective-permute-start.10 = (bf16[1,2,4,2,5,14,256]{6,2,5,4,3,1,0:T(4,128)(2,1)S(1)}, bf16[1,2,4,2,5,14,256]{6,2,5,4,3,1,0:T(4,128)(2,1)S(1)}, u32[]{:S(2)}, u32[]{:S(2)}) collective-permute-start(bf16[1,2,4,2,5,14,256]{6,2,5,4,3,1,0:T(4,128)(2,1)S(1)} %bitcast.143), channel_id=1, source_target_pairs={{0,128},{16,144},{32,160},{48,176},{64,192},{80,208},{96,224},{112... | collective-permute-start | bytes 1720328 | tf_op jit(solution)/shard_map/ppermute | solution.py:15
  222.0 240.2 %collective-permute-start.15 = (bf16[1,2,4,2,5,14,256]{6,2,5,4,3,1,0:T(4,128)(2,1)S(1)}, bf16[1,2,4,2,5,14,256]{6,2,5,4,3,1,0:T(4,128)(2,1)}, u32[]{:S(2)}, u32[]{:S(2)}) collective-permute-start(bf16[1,2,4,2,5,14,256]{6,2,5,4,3,1,0:T(4,128)(2,1)S(1)} %bitcast.144), channel_id=1, source_target_pairs={{0,128},{16,144},{32,160},{48,176},{64,192},{80,208},{96,224},{112... | collective-permute-start | bytes 1720328 | tf_op jit(solution)/shard_map/ppermute | solution.py:15
  224.0 244.2 %collective-permute-start.6 = (bf16[1,2,4,2,5,14,256]{6,2,5,4,3,1,0:T(4,128)(2,1)S(1)}, bf16[1,2,4,2,5,14,256]{6,2,5,4,3,1,0:T(4,128)(2,1)}, u32[]{:S(2)}, u32[]{:S(2)}) collective-permute-start(bf16[1,2,4,2,5,14,256]{6,2,5,4,3,1,0:T(4,128)(2,1)S(1)} %bitcast.145), channel_id=1, source_target_pairs={{0,256},{16,272},{32,288},{48,304},{64,320},{80,336},{96,352},{112... | collective-permute-start | bytes 1720328 | tf_op jit(solution)/shard_map/ppermute | solution.py:15
  460.3 27.6 %collective-permute-start.11 = (bf16[1,2,4,2,5,14,256]{6,2,5,4,3,1,0:T(4,128)(2,1)S(1)}, bf16[1,2,4,2,5,14,256]{6,2,5,4,3,1,0:T(4,128)(2,1)S(1)}, u32[]{:S(2)}, u32[]{:S(2)}) collective-permute-start(bf16[1,2,4,2,5,14,256]{6,2,5,4,3,1,0:T(4,128)(2,1)S(1)} %bitcast.138), channel_id=1, source_target_pairs={{0,256},{16,272},{32,288},{48,304},{64,320},{80,336},{96,352},{112... | collective-permute-start | bytes 1720328 | tf_op jit(solution)/shard_map/ppermute | solution.py:15
  463.4 8.3 %copy-start.3 = (bf16[2,5,8,256]{3,2,1,0:T(8,128)(2,1)S(1)}, bf16[2,5,8,256]{3,2,1,0:T(8,128)(2,1)}, u32[]{:S(2)}) copy-start(bf16[2,5,8,256]{3,2,1,0:T(8,128)(2,1)} %get-tuple-element.40) | copy-start | bytes 122884
  463.4 32.3 %collective-permute-start.16 = (bf16[1,2,4,2,5,14,256]{6,2,5,4,3,1,0:T(4,128)(2,1)S(1)}, bf16[1,2,4,2,5,14,256]{6,2,5,4,3,1,0:T(4,128)(2,1)S(1)}, u32[]{:S(2)}, u32[]{:S(2)}) collective-permute-start(bf16[1,2,4,2,5,14,256]{6,2,5,4,3,1,0:T(4,128)(2,1)S(1)} %bitcast.139), channel_id=1, source_target_pairs={{0,256},{16,272},{32,288},{48,304},{64,320},{80,336},{96,352},{112... | collective-permute-start | bytes 1720328 | tf_op jit(solution)/shard_map/ppermute | solution.py:15
  469.4 28.5 %collective-permute-start.7 = (bf16[1,2,4,2,5,14,256]{6,2,5,4,3,1,0:T(4,128)(2,1)S(1)}, bf16[1,2,4,2,5,14,256]{6,2,5,4,3,1,0:T(4,128)(2,1)S(1)}, u32[]{:S(2)}, u32[]{:S(2)}) collective-permute-start(bf16[1,2,4,2,5,14,256]{6,2,5,4,3,1,0:T(4,128)(2,1)S(1)} %bitcast.140), channel_id=1, source_target_pairs={{0,16},{16,32},{32,48},{48,64},{64,80},{80,96},{96,112},{112,128},... | collective-permute-start | bytes 1720328 | tf_op jit(solution)/shard_map/ppermute | solution.py:15
  488.0 58.3 %collective-permute-start.12 = (bf16[1,2,4,2,5,14,256]{6,2,5,4,3,1,0:T(4,128)(2,1)S(1)}, bf16[1,2,4,2,5,14,256]{6,2,5,4,3,1,0:T(4,128)(2,1)S(1)}, u32[]{:S(2)}, u32[]{:S(2)}) collective-permute-start(bf16[1,2,4,2,5,14,256]{6,2,5,4,3,1,0:T(4,128)(2,1)S(1)} %bitcast.136), channel_id=1, source_target_pairs={{0,16},{16,32},{32,48},{48,64},{64,80},{80,96},{96,112},{112,128},... | collective-permute-start | bytes 1720328 | tf_op jit(solution)/shard_map/ppermute | solution.py:15
  495.7 56.7 %collective-permute-start.17 = (bf16[1,2,4,2,5,14,256]{6,2,5,4,3,1,0:T(4,128)(2,1)S(1)}, bf16[1,2,4,2,5,14,256]{6,2,5,4,3,1,0:T(4,128)(2,1)S(1)}, u32[]{:S(2)}, u32[]{:S(2)}) collective-permute-start(bf16[1,2,4,2,5,14,256]{6,2,5,4,3,1,0:T(4,128)(2,1)S(1)} %bitcast.133), channel_id=1, source_target_pairs={{0,16},{16,32},{32,48},{48,64},{64,80},{80,96},{96,112},{112,128},... | collective-permute-start | bytes 1720328 | tf_op jit(solution)/shard_map/ppermute | solution.py:15
Sparse Core Ops, SparseCore 0:
  51.2 408.2 all-reduce.2
where the time goes:
time: 573 us; the launch traced here: 572 us
  waiting for transfers between devices  399 us (70%)
  starting transfers between devices  112 us (20%)
  between operations  28.5 us (5%)
  local copies, waits for them, and re-layouts  14.3 us (2%)
  other arithmetic  14.3 us (2%)
    psum x1, waiting for transfers between devices, spread(): return lax.psum(jnp.where(mine, value, jnp.zeros_like(value)), axis)  233 us
    ppermute x16, waiting for transfers between devices, shifted_2(): lax.ppermute(value, axis, [(i, (i + by) % size) for i in range(size)])  163 us
    ppermute x16, starting transfers between devices, shifted_2(): lax.ppermute(value, axis, [(i, (i + by) % size) for i in range(size)])  101 us
  transfers between devices with their start and end apart: 19, of which 12 were waited for; matrix products, arithmetic and copies ran while one was open for 3% of the time, Pallas kernels for 0%

commit v1 on v0

v1 whole, which is shorter than its diff:
```python
import jax
import jax.numpy as jnp
from jax import lax
from jax.experimental import pallas as pl
from jax.experimental.pallas import tpu as pltpu
from jax.sharding import PartitionSpec as P

COEFFS = (0.75, -0.15, 1.0 / 60.0)
NBASE = 3
NCOL = 4
NVAR = 5
CHUNKS = 8
MESH = pl.DeviceIdType.MESH
BF = jnp.bfloat16
F32 = jnp.float32


def build(NY, NZ, NS, interpret=False):
    NT = 2 * NZ
    NH = NY * NT
    HA = NZ // 2
    HB = NZ // 2 - 1
    NO = NY - 1
    RING = CHUNKS + 1
    inject = [0] + [1, 1, 2, 3, 4, 5, 6, 7]

    def kernel(f_hbm, b_hbm, hidx, own, flg, mix, o_hbm, f, bown, hs, hr, gb, qr, bb, *rest):
        g = rest[:CHUNKS]
        (ps, pr, acc, ob, ld_sem, h_send, h_recv, a_send, a_recv, b_send, b_recv, y_send, y_recv,
         x_send, x_recv, p_send, p_recv, o_sem) = rest[CHUNKS:]
        me = lax.axis_index("harm")
        slab = lax.axis_index("slab")
        y, z = me // NZ, me % NZ
        zside = (y * NZ + (z + 1) % NZ, y * NZ + (z + NZ - 1) % NZ)
        yside = [((y + o) % NY) * NZ + z for o in range(1, NY)]
        sside = ((slab + 1) % NS, (slab + NS - 1) % NS)

        loads = [pltpu.make_async_copy(b_hbm.at[0], bown, ld_sem.at[NCOL])]
        loads += [pltpu.make_async_copy(f_hbm.at[:, c], f.at[:, c], ld_sem.at[c]) for c in range(NCOL)]
        for load in loads:
            load.start()

        barrier = pltpu.get_barrier_semaphore()
        for n in zside:
            pl.semaphore_signal(barrier, inc=1, device_id={"harm": n}, device_id_type=MESH)
        for n in yside:
            pl.semaphore_signal(barrier, inc=1, device_id={"harm": n}, device_id_type=MESH)
        for n in sside:
            pl.semaphore_signal(barrier, inc=1, device_id={"slab": n}, device_id_type=MESH)

        row = lax.broadcasted_iota(jnp.int32, (8, 256), 0)

        def pack(c):
            def one(i, _):
                for v in range(NVAR):
                    re = f[i, c, 0, v].astype(F32)
                    im = f[i, c, 1, v].astype(F32)
                    hs[0, c, i, v] = jnp.where(row < 4, pltpu.roll(re, 4, 0), im).astype(BF)
                    hs[1, c, i, v] = jnp.where(row < 4, re, pltpu.roll(im, 4, 0)).astype(BF)
                return 0

            lax.fori_loop(0, 2, one, 0)

        loads[0].wait()
        for half in range(2):
            for r in range(2):
                for v in range(NVAR):
                    gb[z, half, r, v] = bown[r, v, :, 128 * half : 128 * half + 128]
        for c in range(NCOL):
            loads[1 + c].wait()
            pack(c)

        pl.semaphore_wait(barrier, 2 + NO + 2)

        def halo(d, c):
            return pltpu.make_async_remote_copy(
                hs.at[d, c], hr.at[d, c], h_send.at[d, c], h_recv.at[d, c],
                device_id={"slab": sside[d]}, device_id_type=MESH)

        def ring(k, way, hop):
            sign = 1 if (k + way) % 2 == 0 else -1
            origin = (z + NZ - sign * (hop - 1)) % NZ
            buf = gb if k == 0 else g[k - 1]
            send, recv = (a_send, a_recv) if way == 0 else (b_send, b_recv)
            return pltpu.make_async_remote_copy(
                buf.at[origin], buf.at[origin], send.at[k, hop - 1], recv.at[k, hop - 1],
                device_id={"harm": zside[0 if sign == 1 else 1]}, device_id_type=MESH)

        def ring_arrived(k, way, hop):
            sign = 1 if (k + way) % 2 == 0 else -1
            origin = (z + NZ - sign * hop) % NZ
            buf = gb if k == 0 else g[k - 1]
            send, recv = (a_send, a_recv) if way == 0 else (b_send, b_recv)
            pltpu.make_async_remote_copy(
                buf.at[origin], buf.at[origin], send.at[k, hop - 1], recv.at[k, hop - 1],
                device_id={"harm": zside[0 if sign == 1 else 1]}, device_id_type=MESH).wait_recv()

        def base_row(o):
            return pltpu.make_async_remote_copy(
                qr.at[y], qr.at[y], y_send.at[o - 1], y_recv.at[o - 1],
                device_id={"harm": yside[o - 1]}, device_id_type=MESH)

        def base_row_arrived(o):
            src = (y + NY - o) % NY
            pltpu.make_async_remote_copy(
                qr.at[src], qr.at[src], y_send.at[o - 1], y_recv.at[o - 1],
                device_id={"harm": yside[o - 1]}, device_id_type=MESH).wait_recv()

        w = z % 2
        pair = y * NZ + z + 1 - 2 * w

        def base_pair(slot):
            return pltpu.make_async_remote_copy(
                bb.at[slot], bb.at[slot], x_send.at[0], x_recv.at[0],
                device_id={"harm": pair}, device_id_type=MESH)

        def part(q, o):
            return pltpu.make_async_remote_copy(
                ps.at[q, o - 1], pr.at[q, o - 1], p_send.at[q, o - 1], p_recv.at[q, o - 1],
                device_id={"harm": yside[o - 1]}, device_id_type=MESH)

        def out_copy(c):
            return pltpu.make_async_copy(ob.at[:, c], o_hbm.at[:, c], o_sem.at[c])

        def mixed(c):
            weights = [[mix[v, u] for u in range(NVAR)] for v in range(NVAR)]

            def one(i, _):
                for r in range(2):
                    grads = []
                    for v in range(NVAR):
                        a = f[i, c, r, v].astype(F32)
                        prev = hr[0, c, i, v].astype(F32)
                        nxt = hr[1, c, i, v].astype(F32)
                        if r == 0:
                            prev = pltpu.roll(prev, 4, 0)
                        else:
                            nxt = pltpu.roll(nxt, 4, 0)
                        total = None
                        for s in range(1, 4):
                            up = pltpu.roll(jnp.where(row >= s, a, nxt), 8 - s, 0)
                            down = pltpu.roll(jnp.where(row < 8 - s, a, prev), s, 0)
                            right = pltpu.roll(a, 256 - s, 1)
                            left = pltpu.roll(a, s, 1)
                            piece = COEFFS[s - 1] * ((up - down) + (right - left))
                            total = piece if total is None else total + piece
                        grads.append(total)
                    for v in range(NVAR):
                        m = weights[v][0] * grads[0]
                        for u in range(1, NVAR):
                            m = m + weights[v][u] * grads[u]
                        m = m.astype(BF)
                        g[2 * c][z, i, r, v] = m[:, :128]
                        g[2 * c + 1][z, i, r, v] = m[:, 128:]
                return 0

            lax.fori_loop(0, 2, one, 0)

        shift = [hidx[j] & (NH - 1) for j in range(NBASE)]
        whole = [h // NT for h in shift]
        rest_of = [h % NT for h in shift]
        owner_y = [own[j] // NZ for j in range(NBASE)]
        owner_z = [own[j] % NZ for j in range(NBASE)]

        row1 = lax.broadcasted_iota(jnp.int32, (8, 128), 0)
        damp = jnp.zeros((8, 128), F32)
        for r in range(8):
            damp = jnp.where(row1 == r, -2.0 * flg[r].astype(F32), damp)

        def partial(q):
            c, half = q // 2, q % 2
            buf = g[q]

            def one(i, _):
                t = 2 * z + i
                k = y * NT + t
                freq = 0.1 * jnp.where(k < NH // 2, k, k - NH).astype(F32)
                pick = [(t + NT - b) % NT for b in rest_of]
                off = [(a + jnp.where(t < b, 1, 0)) % NY for a, b in zip(whole, rest_of)]
                hot = [[jnp.where(off[j] == o, 1.0, 0.0).astype(F32) for o in range(NY)] for j in range(NBASE)]
                for v in range(NVAR):
                    fre = f[i, c, 0, v, :, 128 * half : 128 * half + 128].astype(F32)
                    fim = f[i, c, 1, v, :, 128 * half : 128 * half + 128].astype(F32)
                    sums_re = [damp * fre - freq * fim] + [None] * NO
                    sums_im = [damp * fim + freq * fre] + [None] * NO
                    for j in range(NBASE):
                        mre = buf[pick[j] // 2, pick[j] % 2, 0, v].astype(F32)
                        mim = buf[pick[j] // 2, pick[j] % 2, 1, v].astype(F32)
                        bre = bb[half, j, 0, v].astype(F32)
                        bim = bb[half, j, 1, v].astype(F32)
                        tre = bre * mre - bim * mim
                        tim = bre * mim + bim * mre
                        for o in range(NY):
                            if sums_re[o] is None:
                                sums_re[o] = hot[j][o] * tre
                                sums_im[o] = hot[j][o] * tim
                            else:
                                sums_re[o] = sums_re[o] + hot[j][o] * tre
                                sums_im[o] = sums_im[o] + hot[j][o] * tim
                    acc[q, i, 0, v] = sums_re[0]
                    acc[q, i, 1, v] = sums_im[0]
                    for o in range(1, NY):
                        ps[q, o - 1, i, 0, v] = sums_re[o].astype(BF)
                        ps[q, o - 1, i, 1, v] = sums_im[o].astype(BF)
                return 0

            lax.fori_loop(0, 2, one, 0)
            for o in range(1, NY):
                part(q, o).start()

        def finish(q):
            c, half = q // 2, q % 2
            for o in range(1, NY):
                part(q, o).wait_recv()

            def one(i, _):
                for r in range(2):
                    for v in range(NVAR):
                        total = acc[q, i, r, v]
                        for o in range(1, NY):
                            total = total + pr[q, o - 1, i, r, v].astype(F32)
                        ob[i, c, r, v, :, 128 * half : 128 * half + 128] = total.astype(BF)
                return 0

            lax.fori_loop(0, 2, one, 0)
            if half == 1:
                out_copy(c).start()

        for c in range(NCOL):
            halo(0, c).start()
            halo(1, c).start()
            if c == 0:
                ring(0, 0, 1).start()
                ring(0, 1, 1).start()

        done_p, done_f, ready_p, mixed_c = 0, 0, [], 0
        lag = 2
        p_tick = {}
        tick = 0
        base_tick = HA
        while done_f < CHUNKS:
            tick += 1
            for k in range(RING):
                hop = tick - inject[k]
                if 1 <= hop <= HA:
                    ring_arrived(k, 0, hop)
                    if hop < HA:
                        ring(k, 0, hop + 1).start()
                if 1 <= hop <= HB:
                    ring_arrived(k, 1, hop)
                    if hop < HB:
                        ring(k, 1, hop + 1).start()
            for k in range(1, RING):
                if inject[k] == tick:
                    c = (k - 1) // 2
                    if c >= mixed_c:
                        halo(0, c).wait_recv()
                        halo(1, c).wait_recv()
                        mixed(c)
                        mixed_c = c + 1
                    ring(k, 0, 1).start()
                    ring(k, 1, 1).start()
            if tick == base_tick:
                for j in range(NBASE):
                    for r in range(2):
                        for v in range(NVAR):
                            qr[y, j, r, v] = gb[owner_z[j], w, r, v]
                for o in range(1, NY):
                    base_row(o).start()
            if tick == base_tick + 1:
                for o in range(1, NY):
                    base_row_arrived(o)
                for j in range(NBASE):
                    for r in range(2):
                        for v in range(NVAR):
                            bb[w, j, r, v] = qr[owner_y[j], j, r, v]
                base_pair(w).start()
            if tick == base_tick + 2:
                base_pair(1 - w).wait_recv()
            if tick >= base_tick + 2:
                while done_p < CHUNKS and inject[done_p + 1] + HA <= tick:
                    partial(done_p)
                    p_tick[done_p] = tick
                    done_p += 1
            while done_f < done_p and (p_tick[done_f] + lag <= tick or done_p == CHUNKS):
                finish(done_f)
                done_f += 1

        for c in range(NCOL):
            halo(0, c).wait_send()
            halo(1, c).wait_send()
        for k in range(RING):
            for hop in range(1, HA + 1):
                ring(k, 0, hop).wait_send()
            for hop in range(1, HB + 1):
                ring(k, 1, hop).wait_send()
        for o in range(1, NY):
            base_row(o).wait_send()
        base_pair(w).wait_send()
        for q in range(CHUNKS):
            for o in range(1, NY):
                part(q, o).wait_send()
        for c in range(NCOL):
            out_copy(c).wait()

    block = (2, 2, NVAR, 8, 128)
    dma = pltpu.SemaphoreType.DMA
    scratch = [
        pltpu.VMEM((2, NCOL, 2, NVAR, 8, 256), BF),
        pltpu.VMEM((2, NVAR, 8, 256), BF),
        pltpu.VMEM((2, NCOL, 2, NVAR, 8, 256), BF),
        pltpu.VMEM((2, NCOL, 2, NVAR, 8, 256), BF),
        pltpu.VMEM((NZ, 2, 2, NVAR, 8, 128), BF),
        pltpu.VMEM((NY, NBASE, 2, NVAR, 8, 128), BF),
        pltpu.VMEM((2, NBASE, 2, NVAR, 8, 128), BF),
    ]
    scratch += [pltpu.VMEM((NZ,) + block, BF) for _ in range(CHUNKS)]
    scratch += [
        pltpu.VMEM((CHUNKS, NO) + block, BF),
        pltpu.VMEM((CHUNKS, NO) + block, BF),
        pltpu.VMEM((CHUNKS,) + block, F32),
        pltpu.VMEM((2, NCOL, 2, NVAR, 8, 256), BF),
        dma((NCOL + 1,)),
        dma((2, NCOL)), dma((2, NCOL)),
        dma((RING, HA)), dma((RING, HA)),
        dma((RING, HB)), dma((RING, HB)),
        dma((NO,)), dma((NO,)),
        dma((1,)), dma((1,)),
        dma((CHUNKS, NO)), dma((CHUNKS, NO)),
        dma((NCOL,)),
    ]
    smem = pl.BlockSpec(memory_space=pltpu.SMEM)
    hbm = pl.BlockSpec(memory_space=pl.ANY)

    def call(fields, base_store, harmonic_index, owners, sponge_flags, mixing):
        return pl.pallas_call(
            kernel,
            out_shape=jax.ShapeDtypeStruct(fields.shape, BF),
            in_specs=[hbm, hbm, smem, smem, smem, smem],
            out_specs=hbm,
            scratch_shapes=scratch,
            compiler_params=pltpu.CompilerParams(collective_id=0, has_side_effects=True),
            name="resolvent",
            interpret=interpret,
        )(fields, base_store, harmonic_index, owners, sponge_flags, mixing)

    return call


def wrap(mesh, call):
    return jax.shard_map(
        call,
        mesh=mesh,
        in_specs=(
            P("harm", None, None, None, "slab", None),
            P("harm", None, None, "slab", None),
            P(),
            P(),
            P("slab"),
            P(),
        ),
        out_specs=P("harm", None, None, None, "slab", None),
        check_vma=False,
    )


def solution(mesh):
    return wrap(mesh, build(4, mesh.shape["harm"] // 4, mesh.shape["slab"]))
```

time: 573 us -> 75.1 us (0.13)
  waiting for transfers between devices: 399 us -> 0 us
  starting transfers between devices: 112 us -> 0 us
  Pallas kernels: 0 us -> 73.1 us
  between operations: 28.5 us -> 0.01 us
  other arithmetic: 14.3 us -> 0 us
  local copies, waits for them, and re-layouts: 14.3 us -> 1.72 us
    psum x1 -> x0, waiting for transfers between devices: 233 us -> none  [spread(): return lax.psum(jnp.where(mine, value, jnp.zeros_like(value)), axis)]
    ppermute x18 -> x0, waiting for transfers between devices: 166 us -> none  [the longest x16 163 us: shifted_2(): lax.ppermute(value, axis, [(i, (i + by) % size) for i in range(size)])]
    ppermute x18 -> x0, starting transfers between devices: 112 us -> none  [the longest x16 101 us: shifted_2(): lax.ppermute(value, axis, [(i, (i + by) % size) for i in range(size)])]
    pallas_call x0 -> x1, Pallas kernels: none -> 73.1 us  [call(): pl.pallas_call(kernel, out_shape=jax.ShapeDtypeStruct(fields.shape, BF),...]
    slice x24 -> x0, local copies, waits for them, and re-layouts: 10.9 us -> none  [the longest x3 6 us: mix_block(): lax.slice_in_dim(source, 3 + shift_by, 3 + shift_by + width, axis=xaxis)]
    select_n x15 -> x0, other arithmetic: 6.64 us -> none  [the longest x13 5.98 us: rotate(): current = jnp.where(taken, moved, current)]
  transfers between devices with their start and end apart: 19 -> 0, of which waited for: 12 -> 0; matrix products, arithmetic and copies ran while one was open for 3% -> 0% of each run, Pallas kernels for 0% -> 0%
where the time goes in v1:
time: 75.1 us; the launch traced here: 74.9 us
  Pallas kernels  73.1 us (97%)
  local copies, waits for them, and re-layouts  1.72 us (2%)
    pallas_call x1, Pallas kernels, call(): pl.pallas_call(kernel, out_shape=jax.ShapeDtypeStruct(fields.shape, BF),...  73.1 us
    unnamed x1, local copies, waits for them, and re-layouts  1.72 us

profile of v1, /device:TPU:8, one launch (start us, length us, event | category | flops | bytes accessed | tf_op | source)
XLA Modules:
  0.0 74.9 jit_solution(14595790858679394922)
XLA Ops:
  0.0 73.1 %resolvent.1 = bf16[2,4,2,5,8,256]{5,4,3,2,1,0:T(8,128)(2,1)} custom-call(bf16[2,4,2,5,8,256]{5,4,3,2,1,0:T(8,128)(2,1)} %f_hbm.1, bf16[1,2,5,8,256]{4,3,2,1,0:T(8,128)(2,1)} %b_hbm.1, s32[3]{0:T(128)} %hidx.1, s32[3]{0:T(128)} %own.1, s32[8]{0:T(128)} %flg.1, f32[5,5]{1,0:T(8,128)} %mix.1), custom_call_target="tpu_custom_call" | custom-call | tf_op jit(solution)/shard_map/resolvent/pallas_call | solution.py:336
  73.1 1.7 %copy.8 = bf16[2,4,2,5,8,256]{5,4,3,2,1,0:T(8,128)(2,1)} copy(bf16[2,4,2,5,8,256]{5,4,3,2,1,0:T(8,128)(2,1)} %resolvent.1) | data formatting | bytes 655360

commit v2 on v1

--- a/solution.py
+++ b/solution.py
@@ -21,13 +21,13 @@
     HA = NZ // 2
     HB = NZ // 2 - 1
     NO = NY - 1
-    RING = CHUNKS + 1
-    inject = [0] + [1, 1, 2, 3, 4, 5, 6, 7]
+    ZSET = (0, 1, 4, 5)
+    YSET = (2, 3, 6, 7)
 
     def kernel(f_hbm, b_hbm, hidx, own, flg, mix, o_hbm, f, bown, hs, hr, gb, qr, bb, *rest):
         g = rest[:CHUNKS]
         (ps, pr, acc, ob, ld_sem, h_send, h_recv, a_send, a_recv, b_send, b_recv, y_send, y_recv,
-         x_send, x_recv, p_send, p_recv, o_sem) = rest[CHUNKS:]
+         x_send, x_recv, p_send, p_recv, o_sem, prod, cz, ra, rb, ra_send, ra_recv, rb_send, rb_recv) = rest[CHUNKS:]
         me = lax.axis_index("harm")
         slab = lax.axis_index("slab")
         y, z = me // NZ, me % NZ
@@ -119,11 +119,51 @@
                 ps.at[q, o - 1], pr.at[q, o - 1], p_send.at[q, o - 1], p_recv.at[q, o - 1],
                 device_id={"harm": yside[o - 1]}, device_id_type=MESH)
 
+        def gather_row(q, o):
+            return pltpu.make_async_remote_copy(
+                g[q].at[y], g[q].at[y], p_send.at[q, o - 1], p_recv.at[q, o - 1],
+                device_id={"harm": yside[o - 1]}, device_id_type=MESH)
+
+        def gather_row_arrived(q, o):
+            src = (y + NY - o) % NY
+            pltpu.make_async_remote_copy(
+                g[q].at[src], g[q].at[src], p_send.at[q, o - 1], p_recv.at[q, o - 1],
+                device_id={"harm": yside[o - 1]}, device_id_type=MESH).wait_recv()
+
+        def ring_sum(q, way, hop):
+            n = YSET.index(q)
+            sign = 1 if (q + way) % 2 == 0 else -1
+            buf, send, recv, hops = (ra, ra_send, ra_recv, HA) if way == 0 else (rb, rb_send, rb_recv, HB)
+            away = (sign * (hops + 1 - hop)) % NZ
+            src = cz.at[n, away - 1] if hop == 1 else buf.at[n, hop - 2]
+            return pltpu.make_async_remote_copy(
+                src, buf.at[n, hop - 1], send.at[n, hop - 1], recv.at[n, hop - 1],
+                device_id={"harm": zside[0 if sign == 1 else 1]}, device_id_type=MESH)
+
+        def ring_sum_step(q, way, hop):
+            n = YSET.index(q)
+            sign = 1 if (q + way) % 2 == 0 else -1
+            buf, hops = (ra, HA) if way == 0 else (rb, HB)
+            away = (sign * (hops + 1 - hop)) % NZ
+            ring_sum(q, way, hop - 1).wait_recv()
+
+            def one(i, _):
+                for r in range(2):
+                    for v in range(NVAR):
+                        buf[n, hop - 2, i, r, v] = (
+                            buf[n, hop - 2, i, r, v].astype(F32) + cz[n, away - 1, i, r, v].astype(F32)
+                        ).astype(BF)
+                return 0
+
+            lax.fori_loop(0, 2, one, 0)
+            ring_sum(q, way, hop).start()
+
         def out_copy(c):
             return pltpu.make_async_copy(ob.at[:, c], o_hbm.at[:, c], o_sem.at[c])
 
         def mixed(c):
             weights = [[mix[v, u] for u in range(NVAR)] for v in range(NVAR)]
+            slot = z if 2 * c in ZSET else y
 
             def one(i, _):
                 for r in range(2):
@@ -150,8 +190,8 @@
                         for u in range(1, NVAR):
                             m = m + weights[v][u] * grads[u]
                         m = m.astype(BF)
-                        g[2 * c][z, i, r, v] = m[:, :128]
-                        g[2 * c + 1][z, i, r, v] = m[:, 128:]
+                        g[2 * c][slot, i, r, v] = m[:, :128]
+                        g[2 * c + 1][slot, i, r, v] = m[:, 128:]
                 return 0
 
             lax.fori_loop(0, 2, one, 0)
@@ -208,23 +248,97 @@
             for o in range(1, NY):
                 part(q, o).start()
 
+        def shares(q):
+            c, half = q // 2, q % 2
+            n = YSET.index(q)
+            buf = g[q]
+            for o in range(1, NY):
+                gather_row_arrived(q, o)
+
+            def products(i, _):
+                for j in range(NBASE):
+                    t = (2 * z + i + rest_of[j]) % NT
+                    src = (y + 2 * NY - whole[j] - jnp.where(t < rest_of[j], 1, 0)) % NY
+                    for v in range(NVAR):
+                        mre = buf[src, i, 0, v].astype(F32)
+                        mim = buf[src, i, 1, v].astype(F32)
+                        bre = bb[half, j, 0, v].astype(F32)
+                        bim = bb[half, j, 1, v].astype(F32)
+                        prod[j, i, 0, v] = bre * mre - bim * mim
+                        prod[j, i, 1, v] = bre * mim + bim * mre
+                return 0
+
+            lax.fori_loop(0, 2, products, 0)
+
+            def taken(away, i):
+                t = 2 * ((z + away) % NZ) + i
+                out = []
+                for j in range(NBASE):
+                    u = (t + NT - rest_of[j]) % NT
+                    out.append(jnp.where(u // 2 == z, u % 2, 2))
+                return out
+
+            def one(e, _):
+                away, i = e // 2, e % 2
+                idx = taken(away, i)
+                for r in range(2):
+                    for v in range(NVAR):
+                        total = prod[0, idx[0], r, v] + prod[1, idx[1], r, v] + prod[2, idx[2], r, v]
+                        cz[n, away - 1, i, r, v] = total.astype(BF)
+                return 0
+
+            lax.fori_loop(2, 2 * NZ, one, 0)
+            ring_sum(q, 0, 1).start()
+            if HB:
+                ring_sum(q, 1, 1).start()
+
+            def here(i, _):
+                idx = taken(0, i)
+                k = y * NT + 2 * z + i
+                freq = 0.1 * jnp.where(k < NH // 2, k, k - NH).astype(F32)
+                for v in range(NVAR):
+                    fre = f[i, c, 0, v, :, 128 * half : 128 * half + 128].astype(F32)
+                    fim = f[i, c, 1, v, :, 128 * half : 128 * half + 128].astype(F32)
+                    own_part = (damp * fre - freq * fim, damp * fim + freq * fre)
+                    for r in range(2):
+                        total = prod[0, idx[0], r, v] + prod[1, idx[1], r, v] + prod[2, idx[2], r, v]
+                        acc[q, i, r, v] = own_part[r] + total
+                return 0
+
+            lax.fori_loop(0, 2, here, 0)
+
         def finish(q):
             c, half = q // 2, q % 2
-            for o in range(1, NY):
-                part(q, o).wait_recv()
+            if q in ZSET:
+                for o in range(1, NY):
+                    part(q, o).wait_recv()
+            else:
+                ring_sum(q, 0, HA).wait_recv()
+                ring_sum(q, 1, HB).wait_recv()
 
             def one(i, _):
                 for r in range(2):
                     for v in range(NVAR):
                         total = acc[q, i, r, v]
-                        for o in range(1, NY):
-                            total = total + pr[q, o - 1, i, r, v].astype(F32)
+                        if q in ZSET:
+                            for o in range(1, NY):
+                                total = total + pr[q, o - 1, i, r, v].astype(F32)
+                        else:
+                            n = YSET.index(q)
+                            total = total + ra[n, HA - 1, i, r, v].astype(F32)
+                            total = total + rb[n, HB - 1, i, r, v].astype(F32)
                         ob[i, c, r, v, :, 128 * half : 128 * half + 128] = total.astype(BF)
                 return 0
 
             lax.fori_loop(0, 2, one, 0)
             if half == 1:
                 out_copy(c).start()
+
+        zero = jnp.zeros((8, 128), F32)
+        for j in range(NBASE):
+            for r in range(2):
+                for v in range(NVAR):
+                    prod[j, 2, r, v] = zero
 
         for c in range(NCOL):
             halo(0, c).start()
@@ -233,63 +347,78 @@
                 ring(0, 0, 1).start()
                 ring(0, 1, 1).start()
 
-        done_p, done_f, ready_p, mixed_c = 0, 0, [], 0
-        lag = 2
-        p_tick = {}
-        tick = 0
-        base_tick = HA
-        while done_f < CHUNKS:
-            tick += 1
-            for k in range(RING):
-                hop = tick - inject[k]
-                if 1 <= hop <= HA:
-                    ring_arrived(k, 0, hop)
-                    if hop < HA:
-                        ring(k, 0, hop + 1).start()
-                if 1 <= hop <= HB:
-                    ring_arrived(k, 1, hop)
-                    if hop < HB:
-                        ring(k, 1, hop + 1).start()
-            for k in range(1, RING):
-                if inject[k] == tick:
-                    c = (k - 1) // 2
-                    if c >= mixed_c:
-                        halo(0, c).wait_recv()
-                        halo(1, c).wait_recv()
-                        mixed(c)
-                        mixed_c = c + 1
-                    ring(k, 0, 1).start()
-                    ring(k, 1, 1).start()
-            if tick == base_tick:
-                for j in range(NBASE):
-                    for r in range(2):
-                        for v in range(NVAR):
-                            qr[y, j, r, v] = gb[owner_z[j], w, r, v]
-                for o in range(1, NY):
-                    base_row(o).start()
-            if tick == base_tick + 1:
-                for o in range(1, NY):
-                    base_row_arrived(o)
-                for j in range(NBASE):
-                    for r in range(2):
-                        for v in range(NVAR):
-                            bb[w, j, r, v] = qr[owner_y[j], j, r, v]
-                base_pair(w).start()
-            if tick == base_tick + 2:
-                base_pair(1 - w).wait_recv()
-            if tick >= base_tick + 2:
-                while done_p < CHUNKS and inject[done_p + 1] + HA <= tick:
-                    partial(done_p)
-                    p_tick[done_p] = tick
-                    done_p += 1
-            while done_f < done_p and (p_tick[done_f] + lag <= tick or done_p == CHUNKS):
-                finish(done_f)
-                done_f += 1
+        def relay(k, hop):
+            if 1 <= hop <= HA:
+                ring_arrived(k, 0, hop)
+                if hop < HA:
+                    ring(k, 0, hop + 1).start()
+            if 1 <= hop <= HB:
+                ring_arrived(k, 1, hop)
+                if hop < HB:
+                    ring(k, 1, hop + 1).start()
+
+        def base_select():
+            for j in range(NBASE):
+                for r in range(2):
+                    for v in range(NVAR):
+                        qr[y, j, r, v] = gb[owner_z[j], w, r, v]
+            for o in range(1, NY):
+                base_row(o).start()
+
+        def base_swap():
+            for o in range(1, NY):
+                base_row_arrived(o)
+            for j in range(NBASE):
+                for r in range(2):
+                    for v in range(NVAR):
+                        bb[w, j, r, v] = qr[owner_y[j], j, r, v]
+            base_pair(w).start()
+
+        for c in range(NCOL):
+            if c % 2 == 0:
+                relay(0, c // 2 + 1)
+            halo(0, c).wait_recv()
+            halo(1, c).wait_recv()
+            mixed(c)
+            for q in (2 * c, 2 * c + 1):
+                if q in ZSET:
+                    ring(q + 1, 0, 1).start()
+                    ring(q + 1, 1, 1).start()
+                else:
+                    for o in range(1, NY):
+                        gather_row(q, o).start()
+        for hop in range(3, HA + 1):
+            relay(0, hop)
+            if hop < HA:
+                for q in ZSET:
+                    relay(q + 1, hop - 2)
+        base_select()
+        rest_hops = list(range(max(1, HA - 2), HA))
+        for q in ZSET:
+            relay(q + 1, rest_hops[0])
+        base_swap()
+        for hop in rest_hops[1:]:
+            for q in ZSET:
+                relay(q + 1, hop)
+        base_pair(1 - w).wait_recv()
+        for n in range(2):
+            for q in YSET[2 * n : 2 * n + 2]:
+                shares(q)
+            for q in ZSET[2 * n : 2 * n + 2]:
+                relay(q + 1, HA)
+                partial(q)
+        for hop in range(2, HA + 1):
+            for q in YSET:
+                ring_sum_step(q, 0, hop)
+                if hop <= HB:
+                    ring_sum_step(q, 1, hop)
+        for q in range(CHUNKS):
+            finish(q)
 
         for c in range(NCOL):
             halo(0, c).wait_send()
             halo(1, c).wait_send()
-        for k in range(RING):
+        for k in (0,) + tuple(q + 1 for q in ZSET):
             for hop in range(1, HA + 1):
                 ring(k, 0, hop).wait_send()
             for hop in range(1, HB + 1):
@@ -297,9 +426,16 @@
         for o in range(1, NY):
             base_row(o).wait_send()
         base_pair(w).wait_send()
-        for q in range(CHUNKS):
+        for q in ZSET:
             for o in range(1, NY):
                 part(q, o).wait_send()
+        for q in YSET:
+            for o in range(1, NY):
+                gather_row(q, o).wait_send()
+            for hop in range(1, HA + 1):
+                ring_sum(q, 0, hop).wait_send()
+            for hop in range(1, HB + 1):
+                ring_sum(q, 1, hop).wait_send()
         for c in range(NCOL):
             out_copy(c).wait()
 
@@ -314,7 +450,7 @@
         pltpu.VMEM((NY, NBASE, 2, NVAR, 8, 128), BF),
         pltpu.VMEM((2, NBASE, 2, NVAR, 8, 128), BF),
     ]
-    scratch += [pltpu.VMEM((NZ,) + block, BF) for _ in range(CHUNKS)]
+    scratch += [pltpu.VMEM((NZ if q in ZSET else NY,) + block, BF) for q in range(CHUNKS)]
     scratch += [
         pltpu.VMEM((CHUNKS, NO) + block, BF),
         pltpu.VMEM((CHUNKS, NO) + block, BF),
@@ -322,12 +458,18 @@
         pltpu.VMEM((2, NCOL, 2, NVAR, 8, 256), BF),
         dma((NCOL + 1,)),
         dma((2, NCOL)), dma((2, NCOL)),
-        dma((RING, HA)), dma((RING, HA)),
-        dma((RING, HB)), dma((RING, HB)),
+        dma((CHUNKS + 1, HA)), dma((CHUNKS + 1, HA)),
+        dma((CHUNKS + 1, HB)), dma((CHUNKS + 1, HB)),
         dma((NO,)), dma((NO,)),
         dma((1,)), dma((1,)),
         dma((CHUNKS, NO)), dma((CHUNKS, NO)),
         dma((NCOL,)),
+        pltpu.VMEM((NBASE, 3, 2, NVAR, 8, 128), F32),
+        pltpu.VMEM((len(YSET), NZ - 1) + block, BF),
+        pltpu.VMEM((len(YSET), HA) + block, BF),
+        pltpu.VMEM((len(YSET), HB) + block, BF),
+        dma((len(YSET), HA)), dma((len(YSET), HA)),
+        dma((len(YSET), HB)), dma((len(YSET), HB)),
     ]
     smem = pl.BlockSpec(memory_space=pltpu.SMEM)
     hbm = pl.BlockSpec(memory_space=pl.ANY)

time: 75.1 us -> 66.5 us (0.89)
  the two profiles are of different devices: /device:TPU:8 before, /device:TPU:24 now
where the time goes in v2:
time: 66.5 us; the launch traced here: 66.3 us
  Pallas kernels  64.6 us (97%)
  local copies, waits for them, and re-layouts  1.72 us (3%)
    pallas_call x1, Pallas kernels, call(): pl.pallas_call(kernel, out_shape=jax.ShapeDtypeStruct(fields.shape, BF),...  64.6 us
    unnamed x1, local copies, waits for them, and re-layouts  1.72 us

profile of v2, /device:TPU:24, one launch (start us, length us, event | category | flops | bytes accessed | tf_op | source)
XLA Modules:
  0.0 66.3 jit_solution(12509340828112797988)
XLA Ops:
  0.0 64.6 %resolvent.1 = bf16[2,4,2,5,8,256]{5,4,3,2,1,0:T(8,128)(2,1)} custom-call(bf16[2,4,2,5,8,256]{5,4,3,2,1,0:T(8,128)(2,1)} %f_hbm.1, bf16[1,2,5,8,256]{4,3,2,1,0:T(8,128)(2,1)} %b_hbm.1, s32[3]{0:T(128)} %hidx.1, s32[3]{0:T(128)} %own.1, s32[8]{0:T(128)} %flg.1, f32[5,5]{1,0:T(8,128)} %mix.1), custom_call_target="tpu_custom_call" | custom-call | tf_op jit(solution)/shard_map/resolvent/pallas_call | solution.py:478
  64.6 1.7 %copy.8 = bf16[2,4,2,5,8,256]{5,4,3,2,1,0:T(8,128)(2,1)} copy(bf16[2,4,2,5,8,256]{5,4,3,2,1,0:T(8,128)(2,1)} %resolvent.1) | data formatting | bytes 655360

commit v3 on v2

--- a/solution.py
+++ b/solution.py
@@ -10,6 +10,8 @@
 NCOL = 4
 NVAR = 5
 CHUNKS = 8
+COLLECT = 13
+SPREAD = 5
 MESH = pl.DeviceIdType.MESH
 BF = jnp.bfloat16
 F32 = jnp.float32
@@ -21,13 +23,17 @@
     HA = NZ // 2
     HB = NZ // 2 - 1
     NO = NY - 1
+    G = NY * NZ
+    TILES = 4 * NVAR
+    ROUNDS = -(-TILES // G)
+    FORWARD = NY == 4
     ZSET = (0, 1, 4, 5)
     YSET = (2, 3, 6, 7)
 
-    def kernel(f_hbm, b_hbm, hidx, own, flg, mix, o_hbm, f, bown, hs, hr, gb, qr, bb, *rest):
+    def kernel(f_hbm, b_hbm, hidx, own, flg, mix, o_hbm, f, bown, bt, hs, hr, pa, pb, *rest):
         g = rest[:CHUNKS]
-        (ps, pr, acc, ob, ld_sem, h_send, h_recv, a_send, a_recv, b_send, b_recv, y_send, y_recv,
-         x_send, x_recv, p_send, p_recv, o_sem, prod, cz, ra, rb, ra_send, ra_recv, rb_send, rb_recv) = rest[CHUNKS:]
+        (ps, pr, acc, ob, ld_sem, h_send, h_recv, a_send, a_recv, b_send, b_recv, t_send, t_recv, u_send, u_recv,
+         p_send, p_recv, o_sem, prod, cz, ra, rb, ra_send, ra_recv, rb_send, rb_recv, f_send) = rest[CHUNKS:]
         me = lax.axis_index("harm")
         slab = lax.axis_index("slab")
         y, z = me // NZ, me % NZ
@@ -35,16 +41,20 @@
         yside = [((y + o) % NY) * NZ + z for o in range(1, NY)]
         sside = ((slab + 1) % NS, (slab + NS - 1) % NS)
 
-        loads = [pltpu.make_async_copy(b_hbm.at[0], bown, ld_sem.at[NCOL])]
+        loads = [pltpu.make_async_copy(b_hbm, bown, ld_sem.at[NCOL])]
         loads += [pltpu.make_async_copy(f_hbm.at[:, c], f.at[:, c], ld_sem.at[c]) for c in range(NCOL)]
         for load in loads:
             load.start()
 
+        def others(act):
+            def one(o, _):
+                act((me + o) % G)
+                return 0
+
+            lax.fori_loop(1, G, one, 0)
+
         barrier = pltpu.get_barrier_semaphore()
-        for n in zside:
-            pl.semaphore_signal(barrier, inc=1, device_id={"harm": n}, device_id_type=MESH)
-        for n in yside:
-            pl.semaphore_signal(barrier, inc=1, device_id={"harm": n}, device_id_type=MESH)
+        others(lambda d: pl.semaphore_signal(barrier, inc=1, device_id={"harm": d}, device_id_type=MESH))
         for n in sside:
             pl.semaphore_signal(barrier, inc=1, device_id={"slab": n}, device_id_type=MESH)
 
@@ -63,14 +73,13 @@
 
         loads[0].wait()
         for half in range(2):
-            for r in range(2):
-                for v in range(NVAR):
-                    gb[z, half, r, v] = bown[r, v, :, 128 * half : 128 * half + 128]
+            for p in range(2 * NVAR):
+                bt[2 * NVAR * half + p] = bown[p, :, 128 * half : 128 * half + 128]
         for c in range(NCOL):
             loads[1 + c].wait()
             pack(c)
 
-        pl.semaphore_wait(barrier, 2 + NO + 2)
+        pl.semaphore_wait(barrier, G - 1 + 2)
 
         def halo(d, c):
             return pltpu.make_async_remote_copy(
@@ -80,7 +89,7 @@
         def ring(k, way, hop):
             sign = 1 if (k + way) % 2 == 0 else -1
             origin = (z + NZ - sign * (hop - 1)) % NZ
-            buf = gb if k == 0 else g[k - 1]
+            buf = g[k]
             send, recv = (a_send, a_recv) if way == 0 else (b_send, b_recv)
             return pltpu.make_async_remote_copy(
                 buf.at[origin], buf.at[origin], send.at[k, hop - 1], recv.at[k, hop - 1],
@@ -89,30 +98,52 @@
         def ring_arrived(k, way, hop):
             sign = 1 if (k + way) % 2 == 0 else -1
             origin = (z + NZ - sign * hop) % NZ
-            buf = gb if k == 0 else g[k - 1]
+            buf = g[k]
             send, recv = (a_send, a_recv) if way == 0 else (b_send, b_recv)
             pltpu.make_async_remote_copy(
                 buf.at[origin], buf.at[origin], send.at[k, hop - 1], recv.at[k, hop - 1],
                 device_id={"harm": zside[0 if sign == 1 else 1]}, device_id_type=MESH).wait_recv()
 
-        def base_row(o):
-            return pltpu.make_async_remote_copy(
-                qr.at[y], qr.at[y], y_send.at[o - 1], y_recv.at[o - 1],
-                device_id={"harm": yside[o - 1]}, device_id_type=MESH)
-
-        def base_row_arrived(o):
-            src = (y + NY - o) % NY
-            pltpu.make_async_remote_copy(
-                qr.at[src], qr.at[src], y_send.at[o - 1], y_recv.at[o - 1],
-                device_id={"harm": yside[o - 1]}, device_id_type=MESH).wait_recv()
-
-        w = z % 2
-        pair = y * NZ + z + 1 - 2 * w
-
-        def base_pair(slot):
-            return pltpu.make_async_remote_copy(
-                bb.at[slot], bb.at[slot], x_send.at[0], x_recv.at[0],
-                device_id={"harm": pair}, device_id_type=MESH)
+        def tile_at(rnd):
+            return SPREAD * me % G + rnd * G
+
+        mine = sum(jnp.where(tile_at(rnd) < TILES, 1, 0) for rnd in range(ROUNDS))
+
+        def tile_in(p):
+            return pltpu.make_async_remote_copy(
+                bt.at[p], pa.at[p // G, me], t_send.at[0], t_recv.at[p // G],
+                device_id={"harm": COLLECT * p % G}, device_id_type=MESH)
+
+        def tile_out(p, d, rnd):
+            return pltpu.make_async_remote_copy(
+                pb.at[p], pb.at[p], u_send.at[rnd, d], u_recv.at[0],
+                device_id={"harm": d}, device_id_type=MESH)
+
+        def bytes_of(ref, sem):
+            pltpu.make_async_copy(ref, ref, sem).wait()
+
+        def all_tiles(ref, sem):
+            for n in range(ROUNDS + 1):
+                pl.when(mine == n)(lambda n=n: bytes_of(ref.at[pl.ds(0, TILES - n)], sem))
+
+        def tiles_start():
+            for p in range(TILES):
+                pl.when(COLLECT * p % G != me)(lambda p=p: tile_in(p).start())
+            collected(keep)
+
+        def collected(act):
+            for rnd in range(ROUNDS):
+                p = tile_at(rnd)
+                pl.when(p < TILES)(lambda p=p, rnd=rnd: act(p, rnd))
+
+        def collect(p, rnd):
+            bytes_of(pa.at[rnd, pl.ds(0, G - 1)], t_recv.at[rnd])
+            for j in range(NBASE):
+                pb[p, j] = pa[rnd, own[j]]
+            others(lambda d: tile_out(p, d, rnd).start())
+
+        def keep(p, rnd):
+            pa[rnd, me] = bt[p]
 
         def part(q, o):
             return pltpu.make_async_remote_copy(
@@ -129,6 +160,28 @@
             pltpu.make_async_remote_copy(
                 g[q].at[src], g[q].at[src], p_send.at[q, o - 1], p_recv.at[q, o - 1],
                 device_id={"harm": yside[o - 1]}, device_id_type=MESH).wait_recv()
+
+        middle = (y == 1) | (y == 2) if FORWARD else False
+
+        def gather_row_each(act):
+            for o in range(1, NY):
+                if FORWARD and o != 2:
+                    pl.when(y != (3 if o == 1 else 0))(lambda o=o: act(o))
+                else:
+                    act(o)
+
+        def handed(q):
+            src = (y + 2) % NY
+            return pltpu.make_async_remote_copy(
+                g[q].at[src], g[q].at[src], f_send.at[q], p_recv.at[q, 2 * (y - 1)],
+                device_id={"harm": (3 * (y - 1)) * NZ + z}, device_id_type=MESH)
+
+        def hand_on(q):
+            if FORWARD:
+                @pl.when(middle)
+                def _():
+                    gather_row_arrived(q, 2)
+                    handed(q).start()
 
         def ring_sum(q, way, hop):
             n = YSET.index(q)
@@ -199,8 +252,6 @@
         shift = [hidx[j] & (NH - 1) for j in range(NBASE)]
         whole = [h // NT for h in shift]
         rest_of = [h % NT for h in shift]
-        owner_y = [own[j] // NZ for j in range(NBASE)]
-        owner_z = [own[j] % NZ for j in range(NBASE)]
 
         row1 = lax.broadcasted_iota(jnp.int32, (8, 128), 0)
         damp = jnp.zeros((8, 128), F32)
@@ -226,8 +277,8 @@
                     for j in range(NBASE):
                         mre = buf[pick[j] // 2, pick[j] % 2, 0, v].astype(F32)
                         mim = buf[pick[j] // 2, pick[j] % 2, 1, v].astype(F32)
-                        bre = bb[half, j, 0, v].astype(F32)
-                        bim = bb[half, j, 1, v].astype(F32)
+                        bre = pb[2 * half * NVAR + v, j].astype(F32)
+                        bim = pb[(2 * half + 1) * NVAR + v, j].astype(F32)
                         tre = bre * mre - bim * mim
                         tim = bre * mim + bim * mre
                         for o in range(NY):
@@ -253,7 +304,10 @@
             n = YSET.index(q)
             buf = g[q]
             for o in range(1, NY):
-                gather_row_arrived(q, o)
+                if FORWARD and o == 2:
+                    pl.when(jnp.logical_not(middle))(lambda: gather_row_arrived(q, 2))
+                else:
+                    gather_row_arrived(q, o)
 
             def products(i, _):
                 for j in range(NBASE):
@@ -262,8 +316,8 @@
                     for v in range(NVAR):
                         mre = buf[src, i, 0, v].astype(F32)
                         mim = buf[src, i, 1, v].astype(F32)
-                        bre = bb[half, j, 0, v].astype(F32)
-                        bim = bb[half, j, 1, v].astype(F32)
+                        bre = pb[2 * half * NVAR + v, j].astype(F32)
+                        bim = pb[(2 * half + 1) * NVAR + v, j].astype(F32)
                         prod[j, i, 0, v] = bre * mre - bim * mim
                         prod[j, i, 1, v] = bre * mim + bim * mre
                 return 0
@@ -344,98 +398,76 @@
             halo(0, c).start()
             halo(1, c).start()
             if c == 0:
-                ring(0, 0, 1).start()
-                ring(0, 1, 1).start()
-
-        def relay(k, hop):
+                tiles_start()
+
+        def relay(q, hop):
             if 1 <= hop <= HA:
-                ring_arrived(k, 0, hop)
+                ring_arrived(q, 0, hop)
                 if hop < HA:
-                    ring(k, 0, hop + 1).start()
+                    ring(q, 0, hop + 1).start()
             if 1 <= hop <= HB:
-                ring_arrived(k, 1, hop)
+                ring_arrived(q, 1, hop)
                 if hop < HB:
-                    ring(k, 1, hop + 1).start()
-
-        def base_select():
-            for j in range(NBASE):
-                for r in range(2):
-                    for v in range(NVAR):
-                        qr[y, j, r, v] = gb[owner_z[j], w, r, v]
-            for o in range(1, NY):
-                base_row(o).start()
-
-        def base_swap():
-            for o in range(1, NY):
-                base_row_arrived(o)
-            for j in range(NBASE):
-                for r in range(2):
-                    for v in range(NVAR):
-                        bb[w, j, r, v] = qr[owner_y[j], j, r, v]
-            base_pair(w).start()
+                    ring(q, 1, hop + 1).start()
 
         for c in range(NCOL):
-            if c % 2 == 0:
-                relay(0, c // 2 + 1)
             halo(0, c).wait_recv()
             halo(1, c).wait_recv()
             mixed(c)
             for q in (2 * c, 2 * c + 1):
                 if q in ZSET:
-                    ring(q + 1, 0, 1).start()
-                    ring(q + 1, 1, 1).start()
+                    ring(q, 0, 1).start()
+                    ring(q, 1, 1).start()
                 else:
-                    for o in range(1, NY):
-                        gather_row(q, o).start()
-        for hop in range(3, HA + 1):
-            relay(0, hop)
-            if hop < HA:
-                for q in ZSET:
-                    relay(q + 1, hop - 2)
-        base_select()
-        rest_hops = list(range(max(1, HA - 2), HA))
-        for q in ZSET:
-            relay(q + 1, rest_hops[0])
-        base_swap()
-        for hop in rest_hops[1:]:
+                    gather_row_each(lambda o, q=q: gather_row(q, o).start())
+        for hop in range(1, HA):
             for q in ZSET:
-                relay(q + 1, hop)
-        base_pair(1 - w).wait_recv()
+                relay(q, hop)
+            if hop == 1:
+                collected(collect)
+                for q in YSET[:2]:
+                    hand_on(q)
+            if hop == 2:
+                for q in YSET[2:]:
+                    hand_on(q)
+        all_tiles(pb, u_recv.at[0])
         for n in range(2):
             for q in YSET[2 * n : 2 * n + 2]:
                 shares(q)
             for q in ZSET[2 * n : 2 * n + 2]:
-                relay(q + 1, HA)
+                relay(q, HA)
                 partial(q)
         for hop in range(2, HA + 1):
             for q in YSET:
                 ring_sum_step(q, 0, hop)
                 if hop <= HB:
                     ring_sum_step(q, 1, hop)
-        for q in range(CHUNKS):
-            finish(q)
-
         for c in range(NCOL):
             halo(0, c).wait_send()
             halo(1, c).wait_send()
-        for k in (0,) + tuple(q + 1 for q in ZSET):
+        for q in ZSET:
             for hop in range(1, HA + 1):
-                ring(k, 0, hop).wait_send()
+                ring(q, 0, hop).wait_send()
             for hop in range(1, HB + 1):
-                ring(k, 1, hop).wait_send()
-        for o in range(1, NY):
-            base_row(o).wait_send()
-        base_pair(w).wait_send()
+                ring(q, 1, hop).wait_send()
+        all_tiles(bt, t_send.at[0])
+        collected(lambda p, rnd: others(lambda d: tile_out(p, d, rnd).wait_send()))
+        for q in YSET:
+            gather_row_each(lambda o, q=q: gather_row(q, o).wait_send())
+            if FORWARD:
+                pl.when(middle)(lambda q=q: handed(q).wait_send())
+            for hop in range(1, HA):
+                ring_sum(q, 0, hop).wait_send()
+                if hop < HB:
+                    ring_sum(q, 1, hop).wait_send()
+        for q in range(CHUNKS):
+            finish(q)
         for q in ZSET:
             for o in range(1, NY):
                 part(q, o).wait_send()
         for q in YSET:
-            for o in range(1, NY):
-                gather_row(q, o).wait_send()
-            for hop in range(1, HA + 1):
-                ring_sum(q, 0, hop).wait_send()
-            for hop in range(1, HB + 1):
-                ring_sum(q, 1, hop).wait_send()
+            ring_sum(q, 0, HA).wait_send()
+            ring_sum(q, 1, HB).wait_send()
         for c in range(NCOL):
             out_copy(c).wait()
 
@@ -443,12 +475,12 @@
     dma = pltpu.SemaphoreType.DMA
     scratch = [
         pltpu.VMEM((2, NCOL, 2, NVAR, 8, 256), BF),
-        pltpu.VMEM((2, NVAR, 8, 256), BF),
+        pltpu.VMEM((2 * NVAR, 8, 256), BF),
+        pltpu.VMEM((TILES, 8, 128), BF),
         pltpu.VMEM((2, NCOL, 2, NVAR, 8, 256), BF),
         pltpu.VMEM((2, NCOL, 2, NVAR, 8, 256), BF),
-        pltpu.VMEM((NZ, 2, 2, NVAR, 8, 128), BF),
-        pltpu.VMEM((NY, NBASE, 2, NVAR, 8, 128), BF),
-        pltpu.VMEM((2, NBASE, 2, NVAR, 8, 128), BF),
+        pltpu.VMEM((ROUNDS, G, 8, 128), BF),
+        pltpu.VMEM((TILES, NBASE, 8, 128), BF),
     ]
     scratch += [pltpu.VMEM((NZ if q in ZSET else NY,) + block, BF) for q in range(CHUNKS)]
     scratch += [
@@ -458,10 +490,10 @@
         pltpu.VMEM((2, NCOL, 2, NVAR, 8, 256), BF),
         dma((NCOL + 1,)),
         dma((2, NCOL)), dma((2, NCOL)),
-        dma((CHUNKS + 1, HA)), dma((CHUNKS + 1, HA)),
-        dma((CHUNKS + 1, HB)), dma((CHUNKS + 1, HB)),
-        dma((NO,)), dma((NO,)),
-        dma((1,)), dma((1,)),
+        dma((CHUNKS, HA)), dma((CHUNKS, HA)),
+        dma((CHUNKS, HB)), dma((CHUNKS, HB)),
+        dma((1,)), dma((ROUNDS,)),
+        dma((ROUNDS, G)), dma((1,)),
         dma((CHUNKS, NO)), dma((CHUNKS, NO)),
         dma((NCOL,)),
         pltpu.VMEM((NBASE, 3, 2, NVAR, 8, 128), F32),
@@ -470,6 +502,7 @@
         pltpu.VMEM((len(YSET), HB) + block, BF),
         dma((len(YSET), HA)), dma((len(YSET), HA)),
         dma((len(YSET), HB)), dma((len(YSET), HB)),
+        dma((CHUNKS,)),
     ]
     smem = pl.BlockSpec(memory_space=pltpu.SMEM)
     hbm = pl.BlockSpec(memory_space=pl.ANY)
@@ -484,7 +517,7 @@
             compiler_params=pltpu.CompilerParams(collective_id=0, has_side_effects=True),
             name="resolvent",
             interpret=interpret,
-        )(fields, base_store, harmonic_index, owners, sponge_flags, mixing)
+        )(fields, base_store.reshape(2 * NVAR, 8, 256), harmonic_index, owners, sponge_flags, mixing)
 
     return call
 

time: 66.5 us -> 60.9 us (0.916)
  Pallas kernels: 64.6 us -> 59 us
    pallas_call x1, Pallas kernels: 64.6 us -> 59 us  [call(): pl.pallas_call(kernel, out_shape=jax.ShapeDtypeStruct(fields.shape, BF),...]
where the time goes in v3:
time: 60.9 us; the launch traced here: 60.7 us
  Pallas kernels  59 us (97%)
  local copies, waits for them, and re-layouts  1.72 us (3%)
    pallas_call x1, Pallas kernels, call(): pl.pallas_call(kernel, out_shape=jax.ShapeDtypeStruct(fields.shape, BF),...  59 us
    unnamed x1, local copies, waits for them, and re-layouts  1.72 us

profile of v3, /device:TPU:24, one launch (start us, length us, event | category | flops | bytes accessed | tf_op | source)
XLA Modules:
  0.0 60.7 jit_solution(3274637725633867754)
XLA Ops:
  0.0 59.0 %resolvent.1 = bf16[2,4,2,5,8,256]{5,4,3,2,1,0:T(8,128)(2,1)} custom-call(bf16[2,4,2,5,8,256]{5,4,3,2,1,0:T(8,128)(2,1)} %f_hbm.1, bf16[10,8,256]{2,1,0:T(8,128)(2,1)} %bitcast.1, s32[3]{0:T(128)} %hidx.1, s32[3]{0:T(128)} %own.1, s32[8]{0:T(128)} %flg.1, f32[5,5]{1,0:T(8,128)} %mix.1), custom_call_target="tpu_custom_call" | custom-call | tf_op jit(solution)/shard_map/resolvent/pallas_call | solution.py:511
  59.0 1.7 %copy.8 = bf16[2,4,2,5,8,256]{5,4,3,2,1,0:T(8,128)(2,1)} copy(bf16[2,4,2,5,8,256]{5,4,3,2,1,0:T(8,128)(2,1)} %resolvent.1) | data formatting | bytes 655360

commit v4 on v3

--- a/solution.py
+++ b/solution.py
@@ -27,8 +27,8 @@
     TILES = 4 * NVAR
     ROUNDS = -(-TILES // G)
     FORWARD = NY == 4
-    ZSET = (0, 1, 4, 5)
-    YSET = (2, 3, 6, 7)
+    ZSET = (0, 1, 3, 4, 5)
+    YSET = (2, 6, 7)
 
     def kernel(f_hbm, b_hbm, hidx, own, flg, mix, o_hbm, f, bown, bt, hs, hr, pa, pb, *rest):
         g = rest[:CHUNKS]
@@ -216,7 +216,7 @@
 
         def mixed(c):
             weights = [[mix[v, u] for u in range(NVAR)] for v in range(NVAR)]
-            slot = z if 2 * c in ZSET else y
+            slots = [z if q in ZSET else y for q in (2 * c, 2 * c + 1)]
 
             def one(i, _):
                 for r in range(2):
@@ -243,8 +243,8 @@
                         for u in range(1, NVAR):
                             m = m + weights[v][u] * grads[u]
                         m = m.astype(BF)
-                        g[2 * c][slot, i, r, v] = m[:, :128]
-                        g[2 * c + 1][slot, i, r, v] = m[:, 128:]
+                        g[2 * c][slots[0], i, r, v] = m[:, :128]
+                        g[2 * c + 1][slots[1], i, r, v] = m[:, 128:]
                 return 0
 
             lax.fori_loop(0, 2, one, 0)
@@ -341,10 +341,14 @@
                         cz[n, away - 1, i, r, v] = total.astype(BF)
                 return 0
 
-            lax.fori_loop(2, 2 * NZ, one, 0)
+            first = (HA, HB if q % 2 else NZ - HB)
+            for away in first:
+                lax.fori_loop(2 * away, 2 * away + 2, one, 0)
             ring_sum(q, 0, 1).start()
-            if HB:
-                ring_sum(q, 1, 1).start()
+            ring_sum(q, 1, 1).start()
+            lo, hi = min(first), max(first) + 1
+            lax.fori_loop(2, 2 * lo, one, 0)
+            lax.fori_loop(2 * hi, 2 * NZ, one, 0)
 
             def here(i, _):
                 idx = taken(0, i)
@@ -434,7 +438,7 @@
         for n in range(2):
             for q in YSET[2 * n : 2 * n + 2]:
                 shares(q)
-            for q in ZSET[2 * n : 2 * n + 2]:
+            for q in ZSET[2 * n : 2 * n + 2 + n]:
                 relay(q, HA)
                 partial(q)
         for hop in range(2, HA + 1):

time: 60.9 us -> 60.3 us (level)
  the two profiles are of different devices: /device:TPU:24 before, /device:TPU:59 now
where the time goes in v4:
time: 60.3 us; the launch traced here: 60.1 us
  Pallas kernels  58.4 us (97%)
  local copies, waits for them, and re-layouts  1.72 us (3%)
    pallas_call x1, Pallas kernels, call(): pl.pallas_call(kernel, out_shape=jax.ShapeDtypeStruct(fields.shape, BF),...  58.4 us
    unnamed x1, local copies, waits for them, and re-layouts  1.72 us

profile of v4, /device:TPU:59, one launch (start us, length us, event | category | flops | bytes accessed | tf_op | source)
XLA Modules:
  0.0 60.1 jit_solution(12838325219254051610)
XLA Ops:
  0.0 58.4 %resolvent.1 = bf16[2,4,2,5,8,256]{5,4,3,2,1,0:T(8,128)(2,1)} custom-call(bf16[2,4,2,5,8,256]{5,4,3,2,1,0:T(8,128)(2,1)} %f_hbm.1, bf16[10,8,256]{2,1,0:T(8,128)(2,1)} %bitcast.1, s32[3]{0:T(128)} %hidx.1, s32[3]{0:T(128)} %own.1, s32[8]{0:T(128)} %flg.1, f32[5,5]{1,0:T(8,128)} %mix.1), custom_call_target="tpu_custom_call" | custom-call | tf_op jit(solution)/shard_map/resolvent/pallas_call | solution.py:515
  58.4 1.7 %copy.8 = bf16[2,4,2,5,8,256]{5,4,3,2,1,0:T(8,128)(2,1)} copy(bf16[2,4,2,5,8,256]{5,4,3,2,1,0:T(8,128)(2,1)} %resolvent.1) | data formatting | bytes 655360

commit v5 on v4

--- a/solution.py
+++ b/solution.py
@@ -164,7 +164,7 @@
         middle = (y == 1) | (y == 2) if FORWARD else False
 
         def gather_row_each(act):
-            for o in range(1, NY):
+            for o in sorted(range(1, NY), key=lambda o: o != 2):
                 if FORWARD and o != 2:
                     pl.when(y != (3 if o == 1 else 0))(lambda o=o: act(o))
                 else:
@@ -296,8 +296,15 @@
                 return 0
 
             lax.fori_loop(0, 2, one, 0)
-            for o in range(1, NY):
-                part(q, o).start()
+            @pl.when(y < NY // 2)
+            def _():
+                for o in range(NO, 0, -1):
+                    part(q, o).start()
+
+            @pl.when(y >= NY // 2)
+            def _():
+                for o in range(1, NY):
+                    part(q, o).start()
 
         def shares(q):
             c, half = q // 2, q % 2

time: 60.3 us -> 60.1 us (level)
  the two profiles are of different devices: /device:TPU:59 before, /device:TPU:5 now
where the time goes in v5:
time: 60.1 us; the launch traced here: 59.8 us
  Pallas kernels  58.1 us (97%)
  local copies, waits for them, and re-layouts  1.72 us (3%)
    pallas_call x1, Pallas kernels, call(): pl.pallas_call(kernel, out_shape=jax.ShapeDtypeStruct(fields.shape, BF),...  58.1 us
    unnamed x1, local copies, waits for them, and re-layouts  1.72 us

profile of v5, /device:TPU:5, one launch (start us, length us, event | category | flops | bytes accessed | tf_op | source)
XLA Modules:
  0.0 59.8 jit_solution(2820264039384911492)
XLA Ops:
  0.0 58.1 %resolvent.1 = bf16[2,4,2,5,8,256]{5,4,3,2,1,0:T(8,128)(2,1)} custom-call(bf16[2,4,2,5,8,256]{5,4,3,2,1,0:T(8,128)(2,1)} %f_hbm.1, bf16[10,8,256]{2,1,0:T(8,128)(2,1)} %bitcast.1, s32[3]{0:T(128)} %hidx.1, s32[3]{0:T(128)} %own.1, s32[8]{0:T(128)} %flg.1, f32[5,5]{1,0:T(8,128)} %mix.1), custom_call_target="tpu_custom_call" | custom-call | tf_op jit(solution)/shard_map/resolvent/pallas_call | solution.py:522
  58.1 1.7 %copy.8 = bf16[2,4,2,5,8,256]{5,4,3,2,1,0:T(8,128)(2,1)} copy(bf16[2,4,2,5,8,256]{5,4,3,2,1,0:T(8,128)(2,1)} %resolvent.1) | data formatting | bytes 655360
